TPU v7x, 32 devices: a whole 2x2x4 slice. The times are simulated.
32 devices in a mesh: dp: 8 (over y, x, core), mp: 4 (over z).
Axes of the slice: x: 2, y: 2, z: 4, core: 2. Of those that a mesh axis runs over, the one named last changes fastest.
Arguments:
- tokens: bfloat16 [8192, 1536], P(('dp', 'mp')), may hold values from -6 to 6
- cotangent: bfloat16 [8192, 1536], P(('dp', 'mp')), may hold values from -6 to 6
- lengths: int32 [8, 8], P('dp'), may hold values from 1 to 512, 1024 in all within a row
- granularity: int32 [8], P('dp'), may hold values from 0 to 3
- ln1_gain: float32 [1536], replicated, may hold values from 0.5 to 1.5
- ln1_bias: float32 [1536], replicated, may hold values from -1.5 to 1.5
- w_qkv: bfloat16 [1536, 3, 1536], P('dp', None, 'mp'), may hold values from -0.21875 to 0.21875
- w_out: bfloat16 [1536, 1536], P(('mp', 'dp')), may hold values from -0.4375 to 0.4375
- ln2_gain: float32 [1536], replicated, may hold values from 0.5 to 1.5
- ln2_bias: float32 [1536], replicated, may hold values from -1.5 to 1.5
- w_up: bfloat16 [1536, 6144], P('dp', 'mp'), may hold values from -0.15625 to 0.15625
- w_down: bfloat16 [6144, 1536], P(('mp', 'dp')), may hold values from -0.15625 to 0.15625
Outputs:
- output: bfloat16 [8192, 1536], P(('dp', 'mp'))
- input_grad: bfloat16 [8192, 1536], P(('dp', 'mp'))
- grad_ln1_gain: float32 [1536], replicated
- grad_ln1_bias: float32 [1536], replicated
- grad_w_qkv: float32 [1536, 3, 1536], P('dp', None, 'mp')
- grad_w_out: float32 [1536, 1536], P(('mp', 'dp'))
- grad_ln2_gain: float32 [1536], replicated
- grad_ln2_bias: float32 [1536], replicated
- grad_w_up: float32 [1536, 6144], P('dp', 'mp')
- grad_w_down: float32 [6144, 1536], P(('mp', 'dp'))
Inputs may be any that keep to these rules, and one draw needn't show every extreme that they name: Row i lists the lengths of the 8 sequences packed in order into batch piece i; each row sums to 1024 and its longest sequence has exactly 512 tokens. Batch piece i uses the first 768 * 2^g hidden units of the feed-forward layer, g = granularity[i].
All inputs are finite; a program needn't handle non-finite values.
Results may differ from a plain program's by a relative error of at most 0.018.
Values may be sent and summed in bfloat16 or wider, within the bound.
No kernel may reach another device: no remote copies, remote signals or barrier semaphores. Data moves between devices by JAX's collectives and lax.ppermute only.
A program may use at most 128 MiB of HBM per device.

v0:
```python
import math
import jax
import jax.numpy as jnp
from jax import lax
from jax.sharding import PartitionSpec as P

HDIM = 128
PREFIX0 = 768
EPSILON = 1e-05
MASKED = -1e30


def piece_layout(seq_lengths, total_rows):
    seg_ends = jnp.cumsum(seq_lengths)
    starts = seg_ends - seq_lengths
    places = jnp.arange(total_rows, dtype=jnp.int32)
    seg_ids = jnp.sum((places[:, None] >= seg_ends[None, :]).astype(jnp.int32), axis=1)
    member = seg_ids[:, None] == jnp.arange(seq_lengths.shape[0], dtype=jnp.int32)[None, :]
    offsets = jnp.sum(jnp.where(member, starts[None, :], 0), axis=1)
    return (seg_ids, places - offsets)


def rotary_tables(positions, head_dim):
    half_dim = head_dim // 2
    frequencies = jnp.exp(
        jnp.arange(half_dim, dtype=jnp.float32) * (-2.0 * math.log(10000.0) / head_dim)
    )
    angles = positions.astype(jnp.float32)[:, None] * frequencies[None, :]
    return (jnp.cos(angles), jnp.sin(angles))


def rotate(values, cosine, sine):
    half_dim = values.shape[-1] // 2
    first_half = values[..., :half_dim]
    second_half = values[..., half_dim:]
    cos_rows = cosine[:, None, :]
    sin_rows = sine[:, None, :]
    return jnp.concatenate(
        [
            first_half * cos_rows - second_half * sin_rows,
            second_half * cos_rows + first_half * sin_rows,
        ],
        axis=-1,
    )


def norm_forward(values, norm_gain, norm_bias):
    center = values - jnp.mean(values, axis=-1, keepdims=True)
    inverse = lax.rsqrt(jnp.mean(center * center, axis=-1, keepdims=True) + EPSILON)
    normalized = center * inverse
    return (normalized * norm_gain + norm_bias, normalized, inverse)


def norm_backward(upstream, normalized, inverse, norm_gain):
    scaled = upstream * norm_gain
    return inverse * (
        scaled
        - jnp.mean(scaled, axis=-1, keepdims=True)
        - normalized * jnp.mean(scaled * normalized, axis=-1, keepdims=True)
    )


def gelu_back(pre_values, upstream):
    return jax.vjp(lambda pre_value: jax.nn.gelu(pre_value, approximate=True), pre_values)[1](
        upstream
    )[0]


def on_device(
    tokens,
    cotangent,
    lengths,
    granularity,
    ln1_gain,
    ln1_bias,
    w_qkv,
    w_out,
    ln2_gain,
    ln2_bias,
    w_up,
    w_down,
):
    mp_count = lax.axis_size("mp")
    mp_index = lax.axis_index("mp")
    wide_qkv, wide_up, wide_out, wide_down = (
        lax.all_gather(w_qkv, "dp", axis=0, tiled=True),
        lax.all_gather(w_up, "dp", axis=0, tiled=True),
        lax.all_gather(w_out, "dp", axis=0, tiled=True),
        lax.all_gather(w_down, "dp", axis=0, tiled=True),
    )
    local_rows = tokens.shape[0]
    total_rows = local_rows * mp_count
    head_width = wide_out.shape[0]
    local_heads = head_width // HDIM
    unit_count = wide_up.shape[1]
    block_rows = min(512, total_rows)
    block_count = total_rows // block_rows
    score_scale = HDIM ** (-0.5)
    seg_ids, positions = piece_layout(lengths[0], total_rows)
    places = jnp.arange(total_rows, dtype=jnp.int32)
    cosine, sine = rotary_tables(positions, HDIM)
    tokens_float = tokens.astype(jnp.float32)
    normed_one, unit_one, inverse_one = norm_forward(tokens_float, ln1_gain, ln1_bias)
    inputs_one = lax.all_gather(normed_one.astype(jnp.bfloat16), "mp", axis=0, tiled=True)
    projected = jnp.einsum("td,dch->tch", inputs_one, wide_qkv, preferred_element_type=jnp.float32)
    projected = projected.reshape(total_rows, 3, local_heads, HDIM)
    queries = rotate(projected[:, 0], cosine, sine).astype(jnp.bfloat16)
    keys_rot = rotate(projected[:, 1], cosine, sine).astype(jnp.bfloat16)
    values_all = projected[:, 2].astype(jnp.bfloat16)

    def block_scores(row_start):
        query_block = lax.dynamic_slice_in_dim(queries, row_start, block_rows, 0)
        seg_block = lax.dynamic_slice_in_dim(seg_ids, row_start, block_rows, 0)
        place_block = row_start + jnp.arange(block_rows, dtype=jnp.int32)
        scores = score_scale * jnp.einsum(
            "qhd,khd->hqk", query_block, keys_rot, preferred_element_type=jnp.float32
        )
        allowed = (seg_block[:, None] == seg_ids[None, :]) & (
            place_block[:, None] >= places[None, :]
        )
        return (jnp.where(allowed[None], scores, MASKED), query_block)

    def attend(block_index):
        scores, query_block = block_scores(block_index * block_rows)
        top_score = jnp.max(scores, axis=-1, keepdims=True)
        exp_scores = jnp.exp(scores - top_score)
        row_total = jnp.sum(exp_scores, axis=-1, keepdims=True)
        soft_weights = (exp_scores / row_total).astype(jnp.bfloat16)
        mixed_block = jnp.einsum(
            "hqk,khd->qhd", soft_weights, values_all, preferred_element_type=jnp.float32
        )
        return (mixed_block, (top_score + jnp.log(row_total))[..., 0])

    mixed_blocks, log_totals = lax.map(attend, jnp.arange(block_count, dtype=jnp.int32))
    mixed_heads = mixed_blocks.reshape(total_rows, head_width).astype(jnp.bfloat16)
    attn_part = jnp.dot(mixed_heads, wide_out, preferred_element_type=jnp.float32)
    resid_one = tokens_float + lax.psum_scatter(
        attn_part.astype(jnp.bfloat16), "mp", scatter_dimension=0, tiled=True
    ).astype(jnp.float32)
    normed_two, unit_two, inverse_two = norm_forward(resid_one, ln2_gain, ln2_bias)
    inputs_two = lax.all_gather(normed_two.astype(jnp.bfloat16), "mp", axis=0, tiled=True)
    prefix = PREFIX0 * jnp.left_shift(jnp.int32(1), granularity[0])
    active_units = jnp.clip(prefix - mp_index * unit_count, 0, unit_count)
    keep_units = (jnp.arange(unit_count, dtype=jnp.int32) < active_units).astype(jnp.float32)
    pre_act = jnp.dot(inputs_two, wide_up, preferred_element_type=jnp.float32)
    hidden_act = (jax.nn.gelu(pre_act, approximate=True) * keep_units).astype(jnp.bfloat16)
    ffn_part = jnp.dot(hidden_act, wide_down, preferred_element_type=jnp.float32)
    output = (
        resid_one
        + lax.psum_scatter(
            ffn_part.astype(jnp.bfloat16), "mp", scatter_dimension=0, tiled=True
        ).astype(jnp.float32)
    ).astype(jnp.bfloat16)
    cot_all = lax.all_gather(cotangent, "mp", axis=0, tiled=True)
    hidden_grad = jnp.einsum("td,sd->ts", cot_all, wide_down, preferred_element_type=jnp.float32)
    pre_grad = (gelu_back(pre_act, hidden_grad) * keep_units).astype(jnp.bfloat16)
    grad_up = jnp.einsum("td,ts->ds", inputs_two, pre_grad, preferred_element_type=jnp.float32)
    grad_down = jnp.einsum("ts,td->sd", hidden_act, cot_all, preferred_element_type=jnp.float32)
    ffn_back_part = jnp.einsum("ts,ds->td", pre_grad, wide_up, preferred_element_type=jnp.float32)
    normed_two_grad = lax.psum_scatter(
        ffn_back_part.astype(jnp.bfloat16), "mp", scatter_dimension=0, tiled=True
    ).astype(jnp.float32)
    resid_grad = cotangent.astype(jnp.float32) + norm_backward(
        normed_two_grad, unit_two, inverse_two, ln2_gain
    )
    gain_two_grad = jnp.sum(normed_two_grad * unit_two, axis=0)
    bias_two_grad = jnp.sum(normed_two_grad, axis=0)
    resid_all = lax.all_gather(resid_grad.astype(jnp.bfloat16), "mp", axis=0, tiled=True)
    grad_out = jnp.einsum("th,td->hd", mixed_heads, resid_all, preferred_element_type=jnp.float32)
    mixed_grad = jnp.einsum(
        "td,hd->th", resid_all, wide_out, preferred_element_type=jnp.float32
    ).astype(jnp.bfloat16)
    mixed_grad = mixed_grad.reshape(total_rows, local_heads, HDIM)

    def attend_back(running, block_index):
        key_sum, value_sum = running
        row_start = block_index * block_rows
        scores, query_block = block_scores(row_start)
        log_block = lax.dynamic_index_in_dim(log_totals, block_index, 0, keepdims=False)
        soft_float = jnp.exp(scores - log_block[..., None])
        grad_block = lax.dynamic_slice_in_dim(mixed_grad, row_start, block_rows, 0)
        prob_grad = jnp.einsum(
            "qhd,khd->hqk", grad_block, values_all, preferred_element_type=jnp.float32
        )
        score_grad = (
            soft_float * (prob_grad - jnp.sum(soft_float * prob_grad, axis=-1, keepdims=True))
        ).astype(jnp.bfloat16)
        query_grad = score_scale * jnp.einsum(
            "hqk,khd->qhd", score_grad, keys_rot, preferred_element_type=jnp.float32
        )
        key_sum = key_sum + score_scale * jnp.einsum(
            "hqk,qhd->khd", score_grad, query_block, preferred_element_type=jnp.float32
        )
        value_sum = value_sum + jnp.einsum(
            "hqk,qhd->khd",
            soft_float.astype(jnp.bfloat16),
            grad_block,
            preferred_element_type=jnp.float32,
        )
        return ((key_sum, value_sum), query_grad)

    zero_heads = jnp.zeros((total_rows, local_heads, HDIM), jnp.float32)
    (key_grad, value_grad), query_grads = lax.scan(
        attend_back, (zero_heads, zero_heads), jnp.arange(block_count, dtype=jnp.int32)
    )
    query_grad_all = query_grads.reshape(total_rows, local_heads, HDIM)
    projected_grad = jnp.stack(
        [
            rotate(query_grad_all, cosine, -sine).reshape(total_rows, head_width),
            rotate(key_grad, cosine, -sine).reshape(total_rows, head_width),
            value_grad.reshape(total_rows, head_width),
        ],
        axis=1,
    ).astype(jnp.bfloat16)
    grad_qkv = jnp.einsum(
        "td,tch->dch", inputs_one, projected_grad, preferred_element_type=jnp.float32
    )
    attn_back_part = jnp.einsum(
        "tch,dch->td", projected_grad, wide_qkv, preferred_element_type=jnp.float32
    )
    normed_one_grad = lax.psum_scatter(
        attn_back_part.astype(jnp.bfloat16), "mp", scatter_dimension=0, tiled=True
    ).astype(jnp.float32)
    input_grad = (
        resid_grad + norm_backward(normed_one_grad, unit_one, inverse_one, ln1_gain)
    ).astype(jnp.bfloat16)
    gain_one_grad = jnp.sum(normed_one_grad * unit_one, axis=0)
    bias_one_grad = jnp.sum(normed_one_grad, axis=0)
    norm_sums = lax.psum((gain_one_grad, bias_one_grad, gain_two_grad, bias_two_grad), ("dp", "mp"))
    grad_qkv_shard, grad_up_shard, grad_out_shard, grad_down_shard = (
        lax.psum_scatter(grad_qkv, "dp", scatter_dimension=0, tiled=True),
        lax.psum_scatter(grad_up, "dp", scatter_dimension=0, tiled=True),
        lax.psum_scatter(grad_out, "dp", scatter_dimension=0, tiled=True),
        lax.psum_scatter(grad_down, "dp", scatter_dimension=0, tiled=True),
    )
    return (
        output,
        input_grad,
        norm_sums[0],
        norm_sums[1],
        grad_qkv_shard,
        grad_out_shard,
        norm_sums[2],
        norm_sums[3],
        grad_up_shard,
        grad_down_shard,
    )


def solution(mesh):
    return jax.shard_map(
        on_device,
        mesh=mesh,
        in_specs=(
            P(("dp", "mp"), None),
            P(("dp", "mp"), None),
            P("dp", None),
            P("dp"),
            P(),
            P(),
            P("dp", None, "mp"),
            P(("mp", "dp"), None),
            P(),
            P(),
            P("dp", "mp"),
            P(("mp", "dp"), None),
        ),
        out_specs=(
            P(("dp", "mp"), None),
            P(("dp", "mp"), None),
            P(),
            P(),
            P("dp", None, "mp"),
            P(("mp", "dp"), None),
            P(),
            P(),
            P("dp", "mp"),
            P(("mp", "dp"), None),
        ),
        check_vma=False,
    )
```

profile of v0, /device:TPU:0, one launch (start us, length us, event | category | flops | bytes accessed | tf_op | source)
XLA Modules:
  0.0 1039.5 jit_solution(4531013267683974176)
XLA Ops:
  17.6 61.3 %all-gather.9.cloned.1.call-done = bf16[1024,1536]{1,0:T(8,128)(2,1)} async-done(((bf16[256,1536]{1,0:T(8,128)(2,1)}), bf16[1024,1536]{1,0:T(8,128)(2,1)}) %all-gather.9.cloned.1.call-update) | async-done | bytes 3145744 | tf_op jit(solution)/shard_map/all_gather | solution.py:104
  78.9 34.6 %all-gather.11.cloned.1.call-done = bf16[1536,3,384]{2,0,1:T(8,128)(2,1)} async-done(((bf16[192,3,384]{2,0,1:T(8,128)(2,1)}), bf16[1536,3,384]{2,0,1:T(8,128)(2,1)}) %all-gather.11.cloned.1.call-update) | async-done | bytes 3538960 | tf_op jit(solution)/shard_map/all_gather | solution.py:86
  113.4 7.0 fusion.49
  132.0 15.6 %while.28 = (s32[]{:T(128)}, bf16[2,512,3,128]{3,1,2,0:T(8,128)(2,1)S(1)}, f32[2,3,512]{2,1,0:T(4,128)S(1)}, s32[2]{0:T(128)S(1)}, s32[1024]{0:T(1024)S(1)}, /*i...) while((s32[]{:T(128)}, ...), condition=%wide.region_8.9_spmd.clone, body=%wide.region_5.8_spmd.clone.sunk | while | flops 825752576 | bytes 23797964 | solution.py:134
  152.3 5.0 convolution_convert_fusion.2
  159.3 58.4 %reduce-scatter.9.cloned.1.call-done = bf16[256,1536]{1,0:T(8,128)(2,1)} async-done(((bf16[1024,1536]{1,0:T(8,128)(2,1)}), bf16[256,1536]{1,0:T(8,128)(2,1)}) %reduce-scatter.9.cloned.1.call-update) | async-done | bytes 786448 | tf_op jit(solution)/shard_map/reduce_scatter | solution.py:137
  222.8 59.9 %all-gather.21.cloned.1.call-done = bf16[1024,1536]{1,0:T(8,128)(2,1)} async-done(((bf16[256,1536]{1,0:T(8,128)(2,1)}), bf16[1024,1536]{1,0:T(8,128)(2,1)}) %all-gather.21.cloned.1.call-update) | async-done | bytes 3145744 | tf_op jit(solution)/shard_map/all_gather | solution.py:154
  282.7 39.3 %all-gather.19.cloned.1.call-done = bf16[1536,1536]{1,0:T(8,128)(2,1)} async-done(((bf16[192,1536]{1,0:T(8,128)(2,1)}), bf16[1536,1536]{1,0:T(8,128)(2,1)}) %all-gather.19.cloned.1.call-update) | async-done | bytes 4718608 | tf_op jit(solution)/shard_map/all_gather | solution.py:89
  322.0 9.8 fusion.84
  331.8 31.1 %all-gather.17.cloned.1.call-done = bf16[1536,1536]{1,0:T(8,128)(2,1)} async-done(((bf16[192,1536]{1,0:T(8,128)(2,1)}), bf16[1536,1536]{1,0:T(8,128)(2,1)}) %all-gather.17.cloned.1.call-update) | async-done | bytes 4718608 | tf_op jit(solution)/shard_map/all_gather | solution.py:87
  362.9 65.7 %all-gather.15.cloned.1.call-done = bf16[1024,1536]{1,0:T(8,128)(2,1)} async-done(((bf16[256,1536]{1,0:T(8,128)(2,1)}), bf16[1024,1536]{1,0:T(8,128)(2,1)}) %all-gather.15.cloned.1.call-update) | async-done | bytes 3145744 | tf_op jit(solution)/shard_map/all_gather | solution.py:141
  428.6 13.7 %fusion.46 = (bf16[1024,1536]{1,0:T(8,128)(2,1)S(1)}, f32[1024,1536]{1,0:T(8,128)}) fusion(f32[1024,1536]{1,0:T(8,128)} %fusion.84, f32[1536]{0:T(1024)S(1)} %fusion.77, bf16[1024,1536]{1,0:T(8,128)(2,1)} %all-gather.15.cloned.1.call-done, bf16[1536,1536]{1,0:T(8,128)(2,1)} %all-gather.17.cloned.1.call-done), kind=kOutput, calls=%fused_computation.58 | convolution fusion | flops 4864868352 | bytes 23599104 | tf_op jit(solution)/shard_map/dot_general | solution.py:145
  443.9 6.5 convolution_convert_fusion
  450.5 59.0 %reduce-scatter.13.cloned.1.call-done = bf16[256,1536]{1,0:T(8,128)(2,1)} async-done(((bf16[1024,1536]{1,0:T(8,128)(2,1)}), bf16[256,1536]{1,0:T(8,128)(2,1)}) %reduce-scatter.13.cloned.1.call-update) | async-done | bytes 786448 | tf_op jit(solution)/shard_map/reduce_scatter | solution.py:160
  514.3 63.4 %all-gather.23.cloned.1.call-done = bf16[1024,1536]{1,0:T(8,128)(2,1)} async-done(((bf16[256,1536]{1,0:T(8,128)(2,1)}), bf16[1024,1536]{1,0:T(8,128)(2,1)}) %all-gather.23.cloned.1.call-update) | async-done | bytes 3145744 | tf_op jit(solution)/shard_map/all_gather | solution.py:168
  577.7 4.5 convolution_convert_fusion.3
  582.2 32.5 %while.29 = (s32[]{:T(128)}, f32[1024,3,128]{0,2,1:T(8,128)S(1)}, f32[1024,3,128]{0,2,1:T(8,128)}, f32[2,512,3,128]{3,1,0,2:T(8,128)}, s32[2]{0:T(128)S(1)}, /*i...) while((s32[]{:T(128)}, f32[1024,3,128]{0,2,1:T(8,128)S(1)}, ...), condition=%wide.region_18.19_spmd.clone, body=%wide.region_16.18_spmd.clone.sunk | while | flops 2040593408 | bytes 91812304 | solution.py:203
  617.9 3.3 subtract_convert_fusion.1
  624.9 7.8 bitcast_convert_fusion
  632.8 10.3 convolution_convert_fusion.1
  643.1 10.1 fusion.86
  653.3 11.0 %fusion.82 = f32[1536,1536]{1,0:T(8,128)} fusion(bf16[1024,1536]{1,0:T(8,128)(2,1)} %all-gather.21.cloned.1.call-done, f32[1024,1536]{1,0:T(8,128)} %get-tuple-element.298, f32[1536]{0:T(1024)S(1)} %fusion.77), kind=kOutput, calls=%fused_computation.145 | convolution fusion | flops 4847566848 | bytes 18880512 | tf_op jit(solution)/shard_map/ts,td->sd/dot_general | solution.py:158
  665.4 4.7 fusion.85
  670.5 9.1 fusion.47
  679.7 12.1 %reduce-scatter.15.cloned.1.call-done = bf16[256,1536]{1,0:T(8,128)(2,1)} async-done(((bf16[1024,1536]{1,0:T(8,128)(2,1)}), bf16[256,1536]{1,0:T(8,128)(2,1)}) %reduce-scatter.15.cloned.1.call-update) | async-done | bytes 786448 | tf_op jit(solution)/shard_map/reduce_scatter | solution.py:221
  693.8 45.5 %all-reduce = (f32[1536]{0:T(1024)}, f32[1536]{0:T(1024)}, f32[1536]{0:T(1024)}, f32[1536]{0:T(1024)}) all-reduce(f32[1536]{0:T(1024)S(1)} %get-tuple-element.226, f32[1536]{0:T(1024)S(1)} %get-tuple-element.231, f32[1536]{0:T(1024)S(1)} %copy-done.27, f32[1536]{0:T(1024)S(1)} %copy-done.28), channel_id=1, replica_groups=mesh['dp'=8,'mp'=4] {'dp','mp'}, use_global_device_ids=true, to_apply=%region_23.24 | all-reduce | flops 6144 | bytes 49152 | tf_op jit(solution)/shard_map/psum | solution.py:229
  739.3 16.0 %reduce-scatter.11.cloned.1.call-done = bf16[256,1536]{1,0:T(8,128)(2,1)} async-done(((bf16[1024,1536]{1,0:T(8,128)(2,1)}), bf16[256,1536]{1,0:T(8,128)(2,1)}) %reduce-scatter.11.cloned.1.call-update) | async-done | bytes 786448 | tf_op jit(solution)/shard_map/reduce_scatter | solution.py:150
  755.4 3.6 fusion.66
  759.0 77.0 %reduce-scatter.21.cloned.1.call-done = f32[192,1536]{1,0:T(8,128)} async-done(((f32[1536,1536]{1,0:T(8,128)}), f32[192,1536]{1,0:T(8,128)}) %reduce-scatter.21.cloned.1.call-update) | async-done | bytes 1179664 | tf_op jit(solution)/shard_map/reduce_scatter | solution.py:232
  836.0 80.4 %reduce-scatter.23.cloned.1.call-done = f32[192,1536]{1,0:T(8,128)} async-done(((f32[1536,1536]{1,0:T(8,128)}), f32[192,1536]{1,0:T(8,128)}) %reduce-scatter.23.cloned.1.call-update) | async-done | bytes 1179664 | tf_op jit(solution)/shard_map/reduce_scatter | solution.py:234
  916.4 46.3 %reduce-scatter.19.cloned.1.call-done = f32[48,1536]{1,0:T(8,128)} async-done(((f32[384,1536]{1,0:T(8,128)}), f32[48,1536]{1,0:T(8,128)}) %reduce-scatter.19.cloned.1.call-update) | async-done | bytes 294928 | tf_op jit(solution)/shard_map/reduce_scatter | solution.py:233
  962.7 69.9 %reduce-scatter.17.cloned.1.call-done = f32[192,3,384]{2,0,1:T(8,128)} async-done(((f32[1536,3,384]{2,0,1:T(8,128)}), f32[192,3,384]{2,0,1:T(8,128)}) %reduce-scatter.17.cloned.1.call-update) | async-done | bytes 884752 | tf_op jit(solution)/shard_map/reduce_scatter | solution.py:231
  (219 shorter events, 91.2 us)
Async XLA Ops:
  7.2 71.7 %all-gather.9.cloned.1.call-start = ((), (), s32[]{:S(2)}) async-start(), calls=%async_computation.8 | async-start | bytes 3932160 | tf_op jit(solution)/shard_map/all_gather | solution.py:104
  10.1 110.3 %copy-start.33 = (f32[256]{0:T(256)}, f32[256]{0:T(256)S(1)}, u32[]{:S(2)}) copy-start(f32[256]{0:T(256)S(1)} %add_rsqrt_fusion.1) | copy-start | bytes 3076
  12.5 100.9 %all-gather.11.cloned.1.call-start = ((), (), s32[]{:S(2)}) async-start(), calls=%async_computation.9 | async-start | bytes 3981312 | tf_op jit(solution)/shard_map/all_gather | solution.py:86
  13.2 139.1 %all-gather.13.cloned.1.call-start = ((), (), s32[]{:S(2)}) async-start(), calls=%async_computation.10 | async-start | bytes 1327104 | tf_op jit(solution)/shard_map/all_gather | solution.py:88
  14.0 203.7 %reduce-scatter.9.cloned.1.call-start = ((), (), s32[]{:S(2)}) async-start(), calls=%async_computation.11 | async-start | bytes 3932160 | tf_op jit(solution)/shard_map/reduce_scatter | solution.py:137
  157.3 60.4 %copy-start = (bf16[256,1536]{1,0:T(8,128)(2,1)S(1)}, bf16[256,1536]{1,0:T(8,128)(2,1)}, u32[]{:S(2)}) copy-start(bf16[256,1536]{1,0:T(8,128)(2,1)} %param.16) | copy-start | bytes 2359300
  157.3 125.4 %all-gather.21.cloned.1.call-start = ((), (), s32[]{:S(2)}) async-start(), calls=%async_computation.16 | async-start | bytes 3932160 | tf_op jit(solution)/shard_map/all_gather | solution.py:154
  157.9 62.9 %copy-start.22 = (f32[1536]{0:T(1024)S(1)}, f32[1536]{0:T(1024)}, u32[]{:S(2)}) copy-start(f32[1536]{0:T(1024)} %param.24) | copy-start | bytes 18436
  157.9 62.9 %copy-start.39 = (f32[1536]{0:T(1024)S(1)}, f32[1536]{0:T(1024)}, u32[]{:S(2)}) copy-start(f32[1536]{0:T(1024)} %param.25) | copy-start | bytes 18436
  157.9 164.1 %all-gather.19.cloned.1.call-start = ((), (), s32[]{:S(2)}) async-start(), calls=%async_computation.14 | async-start | bytes 5308416 | tf_op jit(solution)/shard_map/all_gather | solution.py:89
  158.5 204.4 %all-gather.17.cloned.1.call-start = ((), (), s32[]{:S(2)}) async-start(), calls=%async_computation.13 | async-start | bytes 5308416 | tf_op jit(solution)/shard_map/all_gather | solution.py:87
  159.2 269.3 %all-gather.15.cloned.1.call-start = ((), (), s32[]{:S(2)}) async-start(), calls=%async_computation.12 | async-start | bytes 3932160 | tf_op jit(solution)/shard_map/all_gather | solution.py:141
  219.2 293.0 %copy-start.25 = (f32[256]{0:T(256)}, f32[256]{0:T(256)S(1)}, u32[]{:S(2)}) copy-start(f32[256]{0:T(256)S(1)} %broadcast_multiply_fusion.4) | copy-start | bytes 3076
  220.8 291.4 %copy-start.31 = (f32[256]{0:T(256)}, f32[256]{0:T(256)S(1)}, u32[]{:S(2)}) copy-start(f32[256]{0:T(256)S(1)} %add_rsqrt_fusion) | copy-start | bytes 3076
  222.1 287.4 %reduce-scatter.13.cloned.1.call-start = ((), (), s32[]{:S(2)}) async-start(), calls=%async_computation.17 | async-start | bytes 3932160 | tf_op jit(solution)/shard_map/reduce_scatter | solution.py:160
  428.6 15.4 %copy-start.40 = (bf16[1536,1536]{1,0:T(8,128)(2,1)S(1)}, bf16[1536,1536]{1,0:T(8,128)(2,1)}, u32[]{:S(2)}) copy-start(bf16[1536,1536]{1,0:T(8,128)(2,1)} %all-gather.17.cloned.1.call-done) | copy-start | bytes 14155780
  450.4 127.3 %all-gather.23.cloned.1.call-start = ((), (), s32[]{:S(2)}) async-start(), calls=%async_computation.18 | async-start | bytes 3932160 | tf_op jit(solution)/shard_map/all_gather | solution.py:168
  514.1 177.8 %reduce-scatter.15.cloned.1.call-start = ((), (), s32[]{:S(2)}) async-start(), calls=%async_computation.19 | async-start | bytes 3932160 | tf_op jit(solution)/shard_map/reduce_scatter | solution.py:221
  632.8 122.5 %reduce-scatter.11.cloned.1.call-start = ((), (), s32[]{:S(2)}) async-start(), calls=%async_computation.15 | async-start | bytes 3932160 | tf_op jit(solution)/shard_map/reduce_scatter | solution.py:150
  643.1 192.9 %reduce-scatter.21.cloned.1.call-start = ((), (), s32[]{:S(2)}) async-start(), calls=%async_computation.22 | async-start | bytes 10616832 | tf_op jit(solution)/shard_map/reduce_scatter | solution.py:232
  653.3 263.1 %reduce-scatter.23.cloned.1.call-start = ((), (), s32[]{:S(2)}) async-start(), calls=%async_computation.23 | async-start | bytes 10616832 | tf_op jit(solution)/shard_map/reduce_scatter | solution.py:234
  664.3 298.3 %reduce-scatter.19.cloned.1.call-start = ((), (), s32[]{:S(2)}) async-start(), calls=%async_computation.21 | async-start | bytes 2654208 | tf_op jit(solution)/shard_map/reduce_scatter | solution.py:233
  670.1 362.4 %reduce-scatter.17.cloned.1.call-start = ((), (), s32[]{:S(2)}) async-start(), calls=%async_computation.20 | async-start | bytes 7962624 | tf_op jit(solution)/shard_map/reduce_scatter | solution.py:231
  679.6 14.2 %copy-start.27 = (f32[1536]{0:T(1024)S(1)}, f32[1536]{0:T(1024)}, u32[]{:S(2)}) copy-start(f32[1536]{0:T(1024)} %get-tuple-element.224) | copy-start | bytes 18436
  679.6 75.7 %copy-start.5 = (bf16[256,1536]{1,0:T(8,128)(2,1)S(1)}, bf16[256,1536]{1,0:T(8,128)(2,1)}, u32[]{:S(2)}) copy-start(bf16[256,1536]{1,0:T(8,128)(2,1)} %reduce-scatter.9.cloned.1.call-done) | copy-start | bytes 2359300
  679.6 75.7 %copy-start.7 = (bf16[256,1536]{1,0:T(8,128)(2,1)S(1)}, bf16[256,1536]{1,0:T(8,128)(2,1)}, u32[]{:S(2)}) copy-start(bf16[256,1536]{1,0:T(8,128)(2,1)} %param.17) | copy-start | bytes 2359300
  679.6 75.7 %copy-start.9 = (bf16[256,1536]{1,0:T(8,128)(2,1)S(1)}, bf16[256,1536]{1,0:T(8,128)(2,1)}, u32[]{:S(2)}) copy-start(bf16[256,1536]{1,0:T(8,128)(2,1)} %reduce-scatter.13.cloned.1.call-done) | copy-start | bytes 2359300
  679.6 75.7 %copy-start.23 = (f32[1536]{0:T(1024)S(1)}, f32[1536]{0:T(1024)}, u32[]{:S(2)}) copy-start(f32[1536]{0:T(1024)} %param.24) | copy-start | bytes 18436
  679.6 75.7 %copy-start.26 = (f32[256]{0:T(256)S(1)}, f32[256]{0:T(256)}, u32[]{:S(2)}) copy-start(f32[256]{0:T(256)} %copy-done.25) | copy-start | bytes 3076
  679.7 75.7 %copy-start.32 = (f32[256]{0:T(256)S(1)}, f32[256]{0:T(256)}, u32[]{:S(2)}) copy-start(f32[256]{0:T(256)} %copy-done.31) | copy-start | bytes 3076
  679.7 75.7 %copy-start.36 = (f32[256]{0:T(256)S(1)}, f32[256]{0:T(256)}, u32[]{:S(2)}) copy-start(f32[256]{0:T(256)} %copy-done.35) | copy-start | bytes 3076
  679.7 75.7 %copy-start.38 = (f32[256]{0:T(256)S(1)}, f32[256]{0:T(256)}, u32[]{:S(2)}) copy-start(f32[256]{0:T(256)} %copy-done.37) | copy-start | bytes 3076
  (33 other events, 138.3 us)
Sparse Core Ops, SparseCore 0:
  12.6 66.1 all-gather.8
  80.7 32.6 all-gather.10
  115.3 24.0 all-gather.12
  157.4 60.2 reduce-scatter.8
  219.1 63.5 all-gather.20
  284.4 37.5 all-gather.18
  323.9 38.9 all-gather.16
  365.0 63.4 all-gather.14
  450.5 58.8 reduce-scatter.12
  514.2 63.5 all-gather.22
  632.9 58.8 reduce-scatter.14
  694.0 61.2 reduce-scatter.10
  759.4 76.5 reduce-scatter.20
  839.9 76.4 reduce-scatter.22
  920.2 42.4 reduce-scatter.18
  967.0 65.4 reduce-scatter.16
where the time goes:
time: 1050 us; the launch traced here: 1040 us
  waiting for transfers between devices  778 us (74%)
  matrix products  124 us (12%)
  blocking collectives  45.5 us (4%)
  other arithmetic  42.5 us (4%)
  local copies, waits for them, and re-layouts  26.7 us (3%)
  between operations  15.6 us (1%)
    reduce_scatter x1, waiting for transfers between devices, on_device(): lax.psum_scatter(grad_down, 'dp', scatter_dimension=0, tiled=True)  80.4 us
    reduce_scatter x1, waiting for transfers between devices, on_device(): lax.psum_scatter(grad_up, 'dp', scatter_dimension=0, tiled=True)  77 us
    reduce_scatter x1, waiting for transfers between devices, on_device(): lax.psum_scatter(grad_qkv, 'dp', scatter_dimension=0, tiled=True)  69.9 us
    all_gather x1, waiting for transfers between devices, on_device(): lax.all_gather(normed_two.astype(jnp.bfloat16), 'mp', axis=0, tiled=True)  65.7 us
    all_gather x1, waiting for transfers between devices, on_device(): lax.all_gather(resid_grad.astype(jnp.bfloat16), 'mp', axis=0, tiled=True)  63.4 us
    all_gather x1, waiting for transfers between devices, on_device(): lax.all_gather(normed_one.astype(jnp.bfloat16), 'mp', axis=0, tiled=True)  61.3 us
    all_gather x1, waiting for transfers between devices, on_device(): cot_all = lax.all_gather(cotangent, 'mp', axis=0, tiled=True)  59.9 us
    reduce_scatter x1, waiting for transfers between devices, on_device(): lax.psum_scatter(ffn_back_part.astype(jnp.bfloat16), 'mp', scatter_dimens...  59 us
  transfers between devices with their start and end apart: 16, of which 15 were waited for; matrix products, arithmetic and copies ran while one was open for 10% of the time, Pallas kernels for 0%

commit v1 on v0

--- a/solution.py
+++ b/solution.py
@@ -8,6 +8,23 @@
 PREFIX0 = 768
 EPSILON = 1e-05
 MASKED = -1e30
+
+
+def raise_panels_up(mat):
+    chip_axis = "mp"
+    dev_n = lax.psum(1, axis_name=chip_axis)
+    parts_seen = []
+    for j0 in range(dev_n):
+        parts_seen.append((j0, (j0 + 1) % dev_n))
+    extra = [None] * dev_n
+    extra[dev_n - 1] = mat
+    for i in range(dev_n - 2, -1, -1):
+        extra[i] = lax.ppermute(extra[i + 1], axis_name=chip_axis, perm=parts_seen)
+    val = jnp.concatenate(extra, axis=0)
+    all_rows = lax.axis_index(chip_axis)
+    now = (all_rows + 1) * mat.shape[0]
+    response = jnp.roll(val, now, axis=0)
+    return response
 
 
 def piece_layout(seq_lengths, total_rows):
@@ -151,7 +168,7 @@
             ffn_part.astype(jnp.bfloat16), "mp", scatter_dimension=0, tiled=True
         ).astype(jnp.float32)
     ).astype(jnp.bfloat16)
-    cot_all = lax.all_gather(cotangent, "mp", axis=0, tiled=True)
+    cot_all = raise_panels_up(cotangent)
     hidden_grad = jnp.einsum("td,sd->ts", cot_all, wide_down, preferred_element_type=jnp.float32)
     pre_grad = (gelu_back(pre_act, hidden_grad) * keep_units).astype(jnp.bfloat16)
     grad_up = jnp.einsum("td,ts->ds", inputs_two, pre_grad, preferred_element_type=jnp.float32)

time: 1050 us -> 997 us (0.950)
  waiting for transfers between devices: 778 us -> 711 us
  local copies, waits for them, and re-layouts: 26.7 us -> 39.2 us
    ppermute x0 -> x3, waiting for transfers between devices: none -> 73.5 us  [raise_panels_up(): extra[i] = lax.ppermute(extra[i + 1], axis_name=chip_axis, perm=parts_seen)]
    all_gather x1 -> x0, waiting for transfers between devices: 59.9 us -> none  [on_device(): cot_all = lax.all_gather(cotangent, 'mp', axis=0, tiled=True)]
    all_gather x1, waiting for transfers between devices: 65.7 us -> 24.5 us  [on_device(): lax.all_gather(normed_two.astype(jnp.bfloat16), 'mp', axis=0, tiled=True)]
    all_gather x1, waiting for transfers between devices: 31.1 us -> 0.01 us  [on_device(): lax.all_gather(w_up, 'dp', axis=0, tiled=True)]
    unnamed x78 -> x87, local copies, waits for them, and re-layouts: 10.8 us -> 22.5 us
  transfers between devices with their start and end apart: 16 -> 18, of which waited for: 15 -> 16; matrix products, arithmetic and copies ran while one was open for 10% -> 12% of each run, Pallas kernels for 0% -> 0%
where the time goes in v1:
time: 997 us; the launch traced here: 987 us
  waiting for transfers between devices  711 us (71%)
  matrix products  123 us (12%)
  blocking collectives  45.7 us (5%)
  other arithmetic  43.7 us (4%)
  local copies, waits for them, and re-layouts  39.2 us (4%)
  between operations  15.4 us (2%)
    reduce_scatter x1, waiting for transfers between devices, on_device(): lax.psum_scatter(grad_up, 'dp', scatter_dimension=0, tiled=True)  80.6 us
    reduce_scatter x1, waiting for transfers between devices, on_device(): lax.psum_scatter(grad_down, 'dp', scatter_dimension=0, tiled=True)  76.8 us
    ppermute x3, waiting for transfers between devices, raise_panels_up(): extra[i] = lax.ppermute(extra[i + 1], axis_name=chip_axis, perm=parts_seen)  73.5 us
    reduce_scatter x1, waiting for transfers between devices, on_device(): lax.psum_scatter(grad_qkv, 'dp', scatter_dimension=0, tiled=True)  69.9 us
    all_gather x1, waiting for transfers between devices, on_device(): lax.all_gather(resid_grad.astype(jnp.bfloat16), 'mp', axis=0, tiled=True)  63.4 us
    all_gather x1, waiting for transfers between devices, on_device(): lax.all_gather(normed_one.astype(jnp.bfloat16), 'mp', axis=0, tiled=True)  61.3 us
    reduce_scatter x1, waiting for transfers between devices, on_device(): lax.psum_scatter(ffn_back_part.astype(jnp.bfloat16), 'mp', scatter_dimens...  60.4 us
    reduce_scatter x1, waiting for transfers between devices, on_device(): lax.psum_scatter(attn_part.astype(jnp.bfloat16), 'mp', scatter_dimension=...  59.8 us
  transfers between devices with their start and end apart: 18, of which 16 were waited for; matrix products, arithmetic and copies ran while one was open for 12% of the time, Pallas kernels for 0%

profile of v1, /device:TPU:0, one launch (start us, length us, event | category | flops | bytes accessed | tf_op | source)
XLA Modules:
  0.0 986.9 jit_solution(18360328964080986529)
XLA Ops:
  17.6 61.3 %all-gather.8.cloned.1.call-done = bf16[1024,1536]{1,0:T(8,128)(2,1)} async-done(((bf16[256,1536]{1,0:T(8,128)(2,1)}), bf16[1024,1536]{1,0:T(8,128)(2,1)}) %all-gather.8.cloned.1.call-update) | async-done | bytes 3145744 | tf_op jit(solution)/shard_map/all_gather | solution.py:121
  78.9 34.6 %all-gather.10.cloned.1.call-done = bf16[1536,3,384]{2,0,1:T(8,128)(2,1)} async-done(((bf16[192,3,384]{2,0,1:T(8,128)(2,1)}), bf16[1536,3,384]{2,0,1:T(8,128)(2,1)}) %all-gather.10.cloned.1.call-update) | async-done | bytes 3538960 | tf_op jit(solution)/shard_map/all_gather | solution.py:103
  113.4 7.0 fusion.49
  132.0 15.6 %while.28 = (s32[]{:T(128)}, bf16[2,512,3,128]{3,1,2,0:T(8,128)(2,1)S(1)}, f32[2,3,512]{2,1,0:T(4,128)S(1)}, s32[2]{0:T(128)S(1)}, s32[1024]{0:T(1024)S(1)}, /*i...) while((s32[]{:T(128)}, ...), condition=%wide.region_8.9_spmd.clone, body=%wide.region_5.8_spmd.clone.sunk | while | flops 825752576 | bytes 23797964 | solution.py:151
  152.1 5.0 convolution_convert_fusion.2
  157.8 59.8 %reduce-scatter.9.cloned.1.call-done = bf16[256,1536]{1,0:T(8,128)(2,1)} async-done(((bf16[1024,1536]{1,0:T(8,128)(2,1)}), bf16[256,1536]{1,0:T(8,128)(2,1)}) %reduce-scatter.9.cloned.1.call-update) | async-done | bytes 786448 | tf_op jit(solution)/shard_map/reduce_scatter | solution.py:154
  223.8 20.1 %collective-permute-done = bf16[256,1536]{1,0:T(8,128)(2,1)S(1)} collective-permute-done((bf16[256,1536]{1,0:T(8,128)(2,1)}, bf16[256,1536]{1,0:T(8,128)(2,1)S(1)}, u32[]{:S(2)}, u32[]{:S(2)}) %collective-permute-start) | collective-permute-done | bytes 786464 | tf_op jit(solution)/shard_map/ppermute | solution.py:22
  244.8 20.1 %collective-permute-done.1 = bf16[256,1536]{1,0:T(8,128)(2,1)} collective-permute-done((bf16[256,1536]{1,0:T(8,128)(2,1)S(1)}, bf16[256,1536]{1,0:T(8,128)(2,1)}, u32[]{:S(2)}, u32[]{:S(2)}) %collective-permute-start.1) | collective-permute-done | bytes 786464 | tf_op jit(solution)/shard_map/ppermute | solution.py:22
  265.7 33.3 %collective-permute-done.2 = bf16[256,1536]{1,0:T(8,128)(2,1)} collective-permute-done((bf16[256,1536]{1,0:T(8,128)(2,1)}, bf16[256,1536]{1,0:T(8,128)(2,1)}, u32[]{:S(2)}, u32[]{:S(2)}) %collective-permute-start.2) | collective-permute-done | bytes 786464 | tf_op jit(solution)/shard_map/ppermute | solution.py:22
  311.0 24.5 %all-gather.14.cloned.1.call-done = bf16[1024,1536]{1,0:T(8,128)(2,1)} async-done(((bf16[256,1536]{1,0:T(8,128)(2,1)}), bf16[1024,1536]{1,0:T(8,128)(2,1)}) %all-gather.14.cloned.1.call-update) | async-done | bytes 3145744 | tf_op jit(solution)/shard_map/all_gather | solution.py:158
  335.6 9.7 fusion.91
  345.2 29.4 %all-gather.18.cloned.1.call-done = bf16[1536,1536]{1,0:T(8,128)(2,1)} async-done(((bf16[192,1536]{1,0:T(8,128)(2,1)}), bf16[1536,1536]{1,0:T(8,128)(2,1)}) %all-gather.18.cloned.1.call-update) | async-done | bytes 4718608 | tf_op jit(solution)/shard_map/all_gather | solution.py:106
  374.6 12.0 %fusion.46 = bf16[1024,1536]{1,0:T(8,128)(2,1)S(1)} fusion(f32[1024,1536]{1,0:T(8,128)} %fusion.91, f32[1536]{0:T(1024)S(1)} %fusion.83, bf16[1536,1536]{1,0:T(8,128)(2,1)} %all-gather.18.cloned.1.call-done, bf16[2048,1536]{1,0:T(8,128)(2,1)} %constant_dynamic-update-slice_fusion, s32[]{:T(128)S(6)} %select_n.39), kind=kOutput, calls=%fused_computation.58 | convolution fusion | flops 4864868352 | bytes 17307652 | tf_op jit(solution)/shard_map/td,sd->ts/dot_general | solution.py:172
  388.3 6.5 convolution_convert_fusion
  394.8 60.4 %reduce-scatter.13.cloned.1.call-done = bf16[256,1536]{1,0:T(8,128)(2,1)} async-done(((bf16[1024,1536]{1,0:T(8,128)(2,1)}), bf16[256,1536]{1,0:T(8,128)(2,1)}) %reduce-scatter.13.cloned.1.call-update) | async-done | bytes 786448 | tf_op jit(solution)/shard_map/reduce_scatter | solution.py:177
  461.2 63.4 %all-gather.20.cloned.1.call-done = bf16[1024,1536]{1,0:T(8,128)(2,1)} async-done(((bf16[256,1536]{1,0:T(8,128)(2,1)}), bf16[1024,1536]{1,0:T(8,128)(2,1)}) %all-gather.20.cloned.1.call-update) | async-done | bytes 3145744 | tf_op jit(solution)/shard_map/all_gather | solution.py:185
  524.6 4.5 convolution_convert_fusion.3
  529.1 33.0 %while.29 = (s32[]{:T(128)}, f32[1024,3,128]{0,2,1:T(8,128)S(1)}, f32[1024,3,128]{0,2,1:T(8,128)}, f32[2,512,3,128]{3,1,0,2:T(8,128)}, s32[2]{0:T(128)S(1)}, /*i...) while((s32[]{:T(128)}, f32[1024,3,128]{0,2,1:T(8,128)S(1)}, ...), condition=%wide.region_18.19_spmd.clone, body=%wide.region_16.18_spmd.clone.sunk | while | flops 2040593408 | bytes 91812304 | solution.py:220
  572.1 8.1 bitcast_convert_fusion
  580.3 10.3 %convolution_convert_fusion.1 = bf16[1024,1536]{1,0:T(8,128)(2,1)} fusion(bf16[1536,1536]{1,0:T(8,128)(2,1)} %all-gather.18.cloned.1.call-done, f32[1024,1536]{1,0:T(8,128)} %fusion.91, f32[1536]{0:T(1024)S(1)} %fusion.83), kind=kOutput, calls=%fused_computation.62 | convolution fusion | flops 4849139712 | bytes 14161920 | tf_op jit(solution)/shard_map/dot_general | solution.py:164
  590.6 11.0 %fusion.51 = f32[1536,1536]{1,0:T(8,128)} fusion(bf16[2048,1536]{1,0:T(8,128)(2,1)} %constant_dynamic-update-slice_fusion, s32[]{:T(128)S(6)} %select_n.39, f32[1024,1536]{1,0:T(8,128)} %fusion.91, f32[1536]{0:T(1024)S(1)} %fusion.83), kind=kOutput, calls=%fused_computation.68 | convolution fusion | flops 4847566848 | bytes 18880516 | tf_op jit(solution)/shard_map/ts,td->sd/dot_general | solution.py:175
  601.7 10.4 %fusion.93 = f32[1536,1536]{1,0:T(8,128)} fusion(bf16[1024,1536]{1,0:T(8,128)(2,1)} %all-gather.14.cloned.1.call-done, bf16[1024,1536]{1,0:T(8,128)(2,1)} %copy-done.43), kind=kOutput, calls=%fused_computation.162 | convolution fusion | flops 4831838208 | bytes 15728640 | tf_op jit(solution)/shard_map/td,ts->ds/dot_general | solution.py:174
  613.3 4.7 fusion.92
  618.0 9.1 fusion.47
  627.3 12.0 %reduce-scatter.15.cloned.1.call-done = bf16[256,1536]{1,0:T(8,128)(2,1)} async-done(((bf16[1024,1536]{1,0:T(8,128)(2,1)}), bf16[256,1536]{1,0:T(8,128)(2,1)}) %reduce-scatter.15.cloned.1.call-update) | async-done | bytes 786448 | tf_op jit(solution)/shard_map/reduce_scatter | solution.py:238
  641.2 45.7 %all-reduce = (f32[1536]{0:T(1024)}, f32[1536]{0:T(1024)}, f32[1536]{0:T(1024)}, f32[1536]{0:T(1024)}) all-reduce(f32[1536]{0:T(1024)S(1)} %get-tuple-element.226, f32[1536]{0:T(1024)S(1)} %get-tuple-element.231, f32[1536]{0:T(1024)S(1)} %copy-done.28, f32[1536]{0:T(1024)S(1)} %copy-done.29), channel_id=1, replica_groups=mesh['dp'=8,'mp'=4] {'dp','mp'}, use_global_device_ids=true, to_apply=%region_23.24 | all-reduce | flops 6144 | bytes 49152 | tf_op jit(solution)/shard_map/psum | solution.py:246
  686.9 16.0 %reduce-scatter.11.cloned.1.call-done = bf16[256,1536]{1,0:T(8,128)(2,1)} async-done(((bf16[1024,1536]{1,0:T(8,128)(2,1)}), bf16[256,1536]{1,0:T(8,128)(2,1)}) %reduce-scatter.11.cloned.1.call-update) | async-done | bytes 786448 | tf_op jit(solution)/shard_map/reduce_scatter | solution.py:167
  703.0 3.6 fusion.72
  706.7 76.8 %reduce-scatter.23.cloned.1.call-done = f32[192,1536]{1,0:T(8,128)} async-done(((f32[1536,1536]{1,0:T(8,128)}), f32[192,1536]{1,0:T(8,128)}) %reduce-scatter.23.cloned.1.call-update) | async-done | bytes 1179664 | tf_op jit(solution)/shard_map/reduce_scatter | solution.py:251
  783.5 80.6 %reduce-scatter.21.cloned.1.call-done = f32[192,1536]{1,0:T(8,128)} async-done(((f32[1536,1536]{1,0:T(8,128)}), f32[192,1536]{1,0:T(8,128)}) %reduce-scatter.21.cloned.1.call-update) | async-done | bytes 1179664 | tf_op jit(solution)/shard_map/reduce_scatter | solution.py:249
  864.0 46.3 %reduce-scatter.19.cloned.1.call-done = f32[48,1536]{1,0:T(8,128)} async-done(((f32[384,1536]{1,0:T(8,128)}), f32[48,1536]{1,0:T(8,128)}) %reduce-scatter.19.cloned.1.call-update) | async-done | bytes 294928 | tf_op jit(solution)/shard_map/reduce_scatter | solution.py:250
  910.4 69.9 %reduce-scatter.17.cloned.1.call-done = f32[192,3,384]{2,0,1:T(8,128)} async-done(((f32[1536,3,384]{2,0,1:T(8,128)}), f32[192,3,384]{2,0,1:T(8,128)}) %reduce-scatter.17.cloned.1.call-update) | async-done | bytes 884752 | tf_op jit(solution)/shard_map/reduce_scatter | solution.py:248
  (232 shorter events, 108.5 us)
Async XLA Ops:
  7.2 71.7 %all-gather.8.cloned.1.call-start = ((), (), s32[]{:S(2)}) async-start(), calls=%async_computation.8 | async-start | bytes 3932160 | tf_op jit(solution)/shard_map/all_gather | solution.py:121
  8.6 111.8 %copy-start.30 = (f32[256]{0:T(256)}, f32[256]{0:T(256)S(1)}, u32[]{:S(2)}) copy-start(f32[256]{0:T(256)S(1)} %broadcast_multiply_fusion.5) | copy-start | bytes 3076
  10.1 110.3 %copy-start.34 = (f32[256]{0:T(256)}, f32[256]{0:T(256)S(1)}, u32[]{:S(2)}) copy-start(f32[256]{0:T(256)S(1)} %add_rsqrt_fusion.1) | copy-start | bytes 3076
  12.5 100.9 %all-gather.10.cloned.1.call-start = ((), (), s32[]{:S(2)}) async-start(), calls=%async_computation.9 | async-start | bytes 3981312 | tf_op jit(solution)/shard_map/all_gather | solution.py:103
  13.2 138.9 %all-gather.12.cloned.1.call-start = ((), (), s32[]{:S(2)}) async-start(), calls=%async_computation.10 | async-start | bytes 1327104 | tf_op jit(solution)/shard_map/all_gather | solution.py:105
  14.0 203.6 %reduce-scatter.9.cloned.1.call-start = ((), (), s32[]{:S(2)}) async-start(), calls=%async_computation.11 | async-start | bytes 3932160 | tf_op jit(solution)/shard_map/reduce_scatter | solution.py:154
  157.2 153.9 %all-gather.16.cloned.1.call-start = ((), (), s32[]{:S(2)}) async-start(), calls=%async_computation.13 | async-start | bytes 5308416 | tf_op jit(solution)/shard_map/all_gather | solution.py:104
  157.7 177.8 %all-gather.14.cloned.1.call-start = ((), (), s32[]{:S(2)}) async-start(), calls=%async_computation.12 | async-start | bytes 3932160 | tf_op jit(solution)/shard_map/all_gather | solution.py:158
  219.1 238.7 %copy-start.26 = (f32[256]{0:T(256)}, f32[256]{0:T(256)S(1)}, u32[]{:S(2)}) copy-start(f32[256]{0:T(256)S(1)} %broadcast_multiply_fusion.4) | copy-start | bytes 3076
  220.6 237.1 %copy-start.32 = (f32[256]{0:T(256)}, f32[256]{0:T(256)S(1)}, u32[]{:S(2)}) copy-start(f32[256]{0:T(256)S(1)} %add_rsqrt_fusion) | copy-start | bytes 3076
  222.0 152.6 %all-gather.18.cloned.1.call-start = ((), (), s32[]{:S(2)}) async-start(), calls=%async_computation.14 | async-start | bytes 5308416 | tf_op jit(solution)/shard_map/all_gather | solution.py:106
  222.7 232.4 %reduce-scatter.13.cloned.1.call-start = ((), (), s32[]{:S(2)}) async-start(), calls=%async_computation.16 | async-start | bytes 3932160 | tf_op jit(solution)/shard_map/reduce_scatter | solution.py:177
  222.8 21.2 %collective-permute-start = (bf16[256,1536]{1,0:T(8,128)(2,1)}, bf16[256,1536]{1,0:T(8,128)(2,1)S(1)}, u32[]{:S(2)}, u32[]{:S(2)}) collective-permute-start(bf16[256,1536]{1,0:T(8,128)(2,1)} %param.17), channel_id=1, source_target_pairs={{0,1},{1,2},{2,3},{3,0},{4,5},{5,6},{6,7},{7,4},{8,9},{9,10},{10,1... | collective-permute-start | bytes 2359304 | tf_op jit(solution)/shard_map/ppermute | solution.py:22
  244.8 20.1 %collective-permute-start.1 = (bf16[256,1536]{1,0:T(8,128)(2,1)S(1)}, bf16[256,1536]{1,0:T(8,128)(2,1)}, u32[]{:S(2)}, u32[]{:S(2)}) collective-permute-start(bf16[256,1536]{1,0:T(8,128)(2,1)S(1)} %collective-permute-done), channel_id=1, source_target_pairs={{0,1},{1,2},{2,3},{3,0},{4,5},{5,6},{6,7},{7,4},{8,9},{9,10},{10,1... | collective-permute-start | bytes 2359304 | tf_op jit(solution)/shard_map/ppermute | solution.py:22
  265.0 34.0 %collective-permute-start.2 = (bf16[256,1536]{1,0:T(8,128)(2,1)}, bf16[256,1536]{1,0:T(8,128)(2,1)}, u32[]{:S(2)}, u32[]{:S(2)}) collective-permute-start(bf16[256,1536]{1,0:T(8,128)(2,1)} %collective-permute-done.1), channel_id=1, source_target_pairs={{0,1},{1,2},{2,3},{3,0},{4,5},{5,6},{6,7},{7,4},{8,9},{9,10},{10,1... | collective-permute-start | bytes 2359304 | tf_op jit(solution)/shard_map/ppermute | solution.py:22
  394.7 129.9 %all-gather.20.cloned.1.call-start = ((), (), s32[]{:S(2)}) async-start(), calls=%async_computation.17 | async-start | bytes 3932160 | tf_op jit(solution)/shard_map/all_gather | solution.py:185
  457.7 71.4 %copy-start.36 = (f32[256]{0:T(256)}, f32[256]{0:T(256)S(1)}, u32[]{:S(2)}) copy-start(f32[256]{0:T(256)S(1)} %broadcast_multiply_fusion.2) | copy-start | bytes 3076
  457.8 71.3 %copy-start.38 = (f32[256]{0:T(256)}, f32[256]{0:T(256)S(1)}, u32[]{:S(2)}) copy-start(f32[256]{0:T(256)S(1)} %broadcast_multiply_fusion.3) | copy-start | bytes 3076
  460.9 178.4 %reduce-scatter.15.cloned.1.call-start = ((), (), s32[]{:S(2)}) async-start(), calls=%async_computation.18 | async-start | bytes 3932160 | tf_op jit(solution)/shard_map/reduce_scatter | solution.py:238
  580.2 122.8 %reduce-scatter.11.cloned.1.call-start = ((), (), s32[]{:S(2)}) async-start(), calls=%async_computation.15 | async-start | bytes 3932160 | tf_op jit(solution)/shard_map/reduce_scatter | solution.py:167
  590.6 192.9 %reduce-scatter.23.cloned.1.call-start = ((), (), s32[]{:S(2)}) async-start(), calls=%async_computation.22 | async-start | bytes 10616832 | tf_op jit(solution)/shard_map/reduce_scatter | solution.py:251
  601.7 262.4 %reduce-scatter.21.cloned.1.call-start = ((), (), s32[]{:S(2)}) async-start(), calls=%async_computation.21 | async-start | bytes 10616832 | tf_op jit(solution)/shard_map/reduce_scatter | solution.py:249
  612.2 298.2 %reduce-scatter.19.cloned.1.call-start = ((), (), s32[]{:S(2)}) async-start(), calls=%async_computation.20 | async-start | bytes 2654208 | tf_op jit(solution)/shard_map/reduce_scatter | solution.py:250
  618.0 362.3 %reduce-scatter.17.cloned.1.call-start = ((), (), s32[]{:S(2)}) async-start(), calls=%async_computation.19 | async-start | bytes 7962624 | tf_op jit(solution)/shard_map/reduce_scatter | solution.py:248
  627.2 75.8 %copy-start.5 = (bf16[256,1536]{1,0:T(8,128)(2,1)S(1)}, bf16[256,1536]{1,0:T(8,128)(2,1)}, u32[]{:S(2)}) copy-start(bf16[256,1536]{1,0:T(8,128)(2,1)} %reduce-scatter.9.cloned.1.call-done) | copy-start | bytes 2359300
  627.2 75.8 %copy-start.7 = (bf16[256,1536]{1,0:T(8,128)(2,1)S(1)}, bf16[256,1536]{1,0:T(8,128)(2,1)}, u32[]{:S(2)}) copy-start(bf16[256,1536]{1,0:T(8,128)(2,1)} %param.17) | copy-start | bytes 2359300
  627.2 75.8 %copy-start.8 = (bf16[256,1536]{1,0:T(8,128)(2,1)S(1)}, bf16[256,1536]{1,0:T(8,128)(2,1)}, u32[]{:S(2)}) copy-start(bf16[256,1536]{1,0:T(8,128)(2,1)} %reduce-scatter.13.cloned.1.call-done) | copy-start | bytes 2359300
  627.2 75.8 %copy-start.24 = (f32[1536]{0:T(1024)S(1)}, f32[1536]{0:T(1024)}, u32[]{:S(2)}) copy-start(f32[1536]{0:T(1024)} %param.24) | copy-start | bytes 18436
  627.2 75.8 %copy-start.27 = (f32[256]{0:T(256)S(1)}, f32[256]{0:T(256)}, u32[]{:S(2)}) copy-start(f32[256]{0:T(256)} %copy-done.26) | copy-start | bytes 3076
  627.2 75.8 %copy-start.33 = (f32[256]{0:T(256)S(1)}, f32[256]{0:T(256)}, u32[]{:S(2)}) copy-start(f32[256]{0:T(256)} %copy-done.32) | copy-start | bytes 3076
  627.2 75.8 %copy-start.37 = (f32[256]{0:T(256)S(1)}, f32[256]{0:T(256)}, u32[]{:S(2)}) copy-start(f32[256]{0:T(256)} %copy-done.36) | copy-start | bytes 3076
  627.2 75.8 %copy-start.39 = (f32[256]{0:T(256)S(1)}, f32[256]{0:T(256)}, u32[]{:S(2)}) copy-start(f32[256]{0:T(256)} %copy-done.38) | copy-start | bytes 3076
  (36 other events, 410.6 us)
Sparse Core Ops, SparseCore 0:
  12.6 66.1 all-gather.7
  80.7 32.6 all-gather.9
  115.3 24.0 all-gather.11
  157.3 60.2 reduce-scatter.8
  219.3 38.9 all-gather.15
  260.3 75.2 all-gather.13
  337.4 37.1 all-gather.17
  394.9 60.2 reduce-scatter.12
  461.0 63.5 all-gather.19
  580.3 58.8 reduce-scatter.14
  641.6 61.3 reduce-scatter.10
  706.9 76.5 reduce-scatter.22
  787.5 76.4 reduce-scatter.20
  867.8 42.4 reduce-scatter.18
  914.7 65.4 reduce-scatter.16
